TPU v7x, 256 devices: a whole 4x4x8 slice. The times are simulated.
256 devices in a mesh: seq: 64 (over x, z, core), head: 4 (over y).
Axes of the slice: x: 4, y: 4, z: 8, core: 2. Of those that a mesh axis runs over, the one named last changes fastest.
Arguments:
- query: bfloat16 [16384, 8192], P('seq', 'head'), may hold values from -6 to 6
- key_rows: bfloat16 [16384, 8192], P('seq', 'head'), may hold values from -6 to 6
- value_rows: bfloat16 [16384, 8192], P('seq', 'head'), may hold values from -6 to 6
- head_norm_gain: float32 [8192], P('head'), may hold values from 0.25 to 1.75
- decay_level: int32 [64], P('head'), may hold values from 0 to 11
- routing: int32 [16384, 2], P('seq'), may hold values from 0 to 31, all different within a row; in each aligned block of 256 rows (0 to 255, 256 to 511, ...) at most 24 rows name the same one
Outputs:
- dispatched: bfloat16 [32, 1536, 8192], P('head', 'seq')
Inputs may be any that keep to these rules, and one draw needn't show every extreme that they name: `routing`: each token names 2 different experts; among the 256 tokens of one index of seq no expert is named more than 24 times, and in every draw some expert is named exactly 24 times.
All inputs are finite; a program needn't handle non-finite values.
Results may differ from a plain program's by a relative error of at most 0.0049.
Values may be sent and summed in bfloat16 or wider, within the bound.
A program may use at most 192 MiB of HBM per device.

v0:
```python
import jax
import jax.numpy as jnp
from jax import lax
from jax.sharding import PartitionSpec as P

EXPERTS = 32
CAP = 24


def entering(x, axis, combine, identity):
    peers, mine = (lax.axis_size(axis), lax.axis_index(axis))
    everything = jax.tree.map(lambda part: lax.all_gather(part, axis), x)
    start = jax.tree.map(
        lambda part, zero: jnp.broadcast_to(jnp.asarray(zero, part.dtype), part.shape), x, identity
    )

    def hop(k, before):
        reached = k < mine
        new = combine(before, jax.tree.map(lambda part: part[k], everything))
        return jax.tree.map(lambda a, b: jnp.where(reached, a, b), new, before)

    return lax.fori_loop(0, peers, hop, start)


def combine_states(preceding_blocks, later):
    return (
        preceding_blocks[0] * later[0],
        later[0][:, None, None] * preceding_blocks[1] + later[1],
    )


def on_device(query, key_rows, value_rows, head_norm_gain, decay_level, routing):
    length = query.shape[0]
    features = query.shape[1]
    heads_here = decay_level.shape[0]
    head_size = features // heads_here
    seq_count = lax.axis_size("seq")
    head_count = lax.axis_size("head")
    experts_all = EXPERTS
    capacity = CAP
    rate = jnp.exp2(decay_level.astype(jnp.float32) - 2.0) / (length * seq_count)
    place = jnp.arange(length).astype(jnp.float32)
    query_head_rows = query.reshape(length, heads_here, head_size)
    key_head_rows = key_rows.reshape(length, heads_here, head_size)
    value_heads = value_rows.reshape(length, heads_here, head_size)
    decay_out = jnp.exp(-rate[None, :] * (length - 1.0 - place[:, None]))
    weighted_keys = (key_head_rows.astype(jnp.float32) * decay_out[:, :, None]).astype(jnp.bfloat16)
    local_state = jnp.einsum(
        "lhd,lhe->hde", weighted_keys, value_heads, preferred_element_type=jnp.float32
    )
    block_decay = jnp.exp(-rate * length)
    identity = (jnp.ones_like(block_decay), jnp.zeros_like(local_state))
    prefix_decay, incoming = entering((block_decay, local_state), "seq", combine_states, identity)
    offset = place[:, None] - place[None, :]
    mask_decay = jnp.where(
        (offset >= 0)[None, :, :],
        jnp.exp(-rate[:, None, None] * jnp.maximum(offset, 0.0)[None, :, :]),
        0.0,
    )
    attention_scores = jnp.einsum(
        "bjt,rjt->jbr", query_head_rows, key_head_rows, preferred_element_type=jnp.float32
    )
    weights = (attention_scores * mask_decay).astype(jnp.bfloat16)
    intra = jnp.einsum("hlm,mhe->lhe", weights, value_heads, preferred_element_type=jnp.float32)
    decay_in = jnp.exp(-rate[None, :] * (place[:, None] + 1.0))
    inter = (
        jnp.einsum(
            "lhd,hde->lhe",
            query_head_rows.astype(jnp.float32),
            incoming,
            precision=lax.Precision.HIGHEST,
        )
        * decay_in[:, :, None]
    )
    attended = inter + intra
    scale = lax.rsqrt(jnp.mean(attended * attended, axis=-1, keepdims=True) + 1e-05)
    normed = (attended * scale * head_norm_gain.reshape(heads_here, head_size)[None, :, :]).astype(
        jnp.bfloat16
    )
    normed = normed.reshape(length, features)
    rows_total = routing.shape[0] * routing.shape[1]
    flat_routes = routing.reshape(rows_total)
    onehot = (flat_routes[:, None] == jnp.arange(experts_all)[None, :]).astype(jnp.int32)
    before = jnp.cumsum(onehot, axis=0) - onehot
    slot = jnp.sum(before * onehot, axis=-1)
    token_index = jnp.arange(rows_total) // routing.shape[1]
    per_owner = experts_all // head_count
    quarter = length // head_count
    row_room = quarter * routing.shape[1]
    whole_rows = lax.all_to_all(normed, "head", split_axis=0, concat_axis=1, tiled=True)
    width_all = whole_rows.shape[1]
    me_index = lax.axis_index("head")
    source = token_index // quarter
    owner = flat_routes // per_owner
    category = source * head_count + owner
    cat_hot = (category[:, None] == jnp.arange(head_count * head_count)[None, :]).astype(jnp.int32)
    cat_before = jnp.cumsum(cat_hot, axis=0) - cat_hot
    token_position = jnp.sum(cat_before * cat_hot, axis=-1)
    outbound_index = jnp.where(
        source == me_index, owner * row_room + token_position, head_count * row_room
    )
    send_table = (
        jnp.full((head_count * row_room,), quarter, jnp.int32)
        .at[outbound_index]
        .set(token_index - me_index * quarter, mode="drop")
    )
    padded = jnp.concatenate([whole_rows, jnp.zeros((1, width_all), jnp.bfloat16)], axis=0)
    outgoing = jnp.take(padded, send_table, axis=0).reshape(head_count, row_room, width_all)
    arrived = lax.all_to_all(outgoing, "head", split_axis=0, concat_axis=0, tiled=True)
    arrived = arrived.reshape(head_count * row_room, width_all)
    local_slot = jnp.where(
        owner == me_index,
        (flat_routes - me_index * per_owner) * capacity + slot,
        per_owner * capacity,
    )
    recv_table = (
        jnp.full((per_owner * capacity,), head_count * row_room, jnp.int32)
        .at[local_slot]
        .set(source * row_room + token_position, mode="drop")
    )
    padded_in = jnp.concatenate([arrived, jnp.zeros((1, width_all), jnp.bfloat16)], axis=0)
    dispatched = jnp.take(padded_in, recv_table, axis=0).reshape(per_owner, capacity, width_all)
    return dispatched


def solution(mesh):
    in_specs = (
        P("seq", "head"),
        P("seq", "head"),
        P("seq", "head"),
        P("head"),
        P("head"),
        P("seq", None),
    )
    out_specs = P("head", "seq", None)
    return jax.shard_map(
        on_device, mesh=mesh, in_specs=in_specs, out_specs=out_specs, check_vma=False
    )
```

profile of v0, /device:TPU:1, one launch (start us, length us, event | category | flops | bytes accessed | tf_op | source)
XLA Modules:
  0.0 524.0 jit_solution(457577722527314586)
XLA Ops:
  6.6 1.6 copy.40
  8.1 1.5 copy.41
  13.3 130.1 %all-reduce.2 = f32[1024]{0:T(1024)S(1)} all-reduce(f32[1024]{0:T(1024)S(1)} %get-tuple-element.133), channel_id=2, replica_groups=mesh['seq'=64,'head'=4] {'seq'}, use_global_device_ids=true, to_apply=%add.2 | all-reduce | flops 1024 | bytes 8192
  146.9 107.1 %all-gather.4.cloned.1.call-done = f32[1024,128,128]{2,1,0:T(8,128)} async-done(((f32[16,128,128]{2,1,0:T(8,128)}), f32[1024,128,128]{2,1,0:T(8,128)}) %all-gather.4.cloned.1.call-update) | async-done | bytes 67108880 | tf_op jit(solution)/shard_map/all_gather | solution.py:12
  254.0 95.9 %while.14 = (s32[]{:T(128)}, f32[16,128,128]{2,1,0:T(8,128)S(1)}, s32[]{:T(128)}, f32[64,16]{1,0:T(8,128)S(1)}, f32[64,16,128,128]{3,2,1,0:T(8,128)}, /*index=5*/s32[]{:T(128)}, s32[]{:T(128)}) while((s32[]{:T(128)}, f32[16,128,128]{2,1,0:T(8,128)S(1)}, s32[]{:T(128)}, f32[64,16]{1,0:T(8,128)S(1)}, ...), condition=%wide.region_9.10_spmd.clone, body=%wide.region_8.9_spmd.clone.sunk | while | flops 1048580 | bytes 3146025 | solution.py:22
  255.5 1.5 fusion.53
  257.0 1.5 fusion.53
  280.9 1.5 fusion.53
  309.4 1.5 fusion.53
  337.9 1.5 fusion.53
  349.9 2.4 fusion.4
  352.3 4.9 multiply_reduce_fusion
  357.2 1.9 multiply_convert_fusion.1
  361.5 4.0 all-to-all-start
  365.5 2.4 scatter_custom_fusion.1
  368.0 12.2 %all-to-all-done = bf16[4,64,2048]{2,1,0:T(8,128)(2,1)S(1)} async-done(((bf16[4,64,2048]{2,1,0:T(8,128)(2,1)}), bf16[4,64,2048]{2,1,0:T(8,128)(2,1)S(1)}, u32[]{:S(2)}, u32[]{:S(2)}) %all-to-all-start) | async-done | bytes 1048608 | tf_op jit(solution)/shard_map/all_to_all | solution.py:90
  380.4 7.8 %gather_fusion = bf16[512,8192]{1,0:T(8,128)(2,1)} fusion(bf16[65,8192]{1,0:T(8,128)(2,1)S(1)} %concatenate.6, s32[1024]{0:T(1024)S(1)} %pad_clamp_fusion.1), kind=kCustom, calls=%fused_computation | custom fusion | bytes 16779264 | tf_op jit(solution)/shard_map/jit(_take)/gather | solution.py:108
  388.2 7.5 %broadcast_select_fusion = bf16[4,128,8192]{2,1,0:T(8,128)(2,1)} fusion(bf16[4,128,8192]{2,1,0:T(8,128)(2,1)} %bitcast.91, pred[4,128]{1,0:T(4,128)(4,1)S(1)} %and_bitcast_fusion), kind=kLoop, calls=%fused_computation.7 | loop fusion | flops 4194304 | bytes 16777728 | tf_op jit(solution)/shard_map/jit(_take)/select_n | solution.py:108
  395.6 5.8 %all-to-all-start.1 = ((bf16[4,128,8192]{2,1,0:T(8,128)(2,1)}), bf16[4,128,8192]{2,1,0:T(8,128)(2,1)}, u32[]{:S(2)}, u32[]{:S(2)}) async-start(bf16[4,128,8192]{2,1,0:T(8,128)(2,1)} %broadcast_select_fusion), calls=%async_computation.1 | async-start | bytes 16777216 | tf_op jit(solution)/shard_map/all_to_all | solution.py:109
  401.5 2.4 scatter_custom_fusion
  404.1 89.7 %all-to-all-done.1 = bf16[4,128,8192]{2,1,0:T(8,128)(2,1)} async-done(((bf16[4,128,8192]{2,1,0:T(8,128)(2,1)}), bf16[4,128,8192]{2,1,0:T(8,128)(2,1)}, u32[]{:S(2)}, u32[]{:S(2)}) %all-to-all-start.1) | async-done | bytes 8388640 | tf_op jit(solution)/shard_map/all_to_all | solution.py:109
  493.8 7.9 %concatenate.7 = bf16[513,8192]{1,0:T(8,128)(2,1)} pad(bf16[512,8192]{1,0:T(8,128)(2,1)} %bitcast.14, bf16[]{:T(256)} %constant.152.clone.1), padding=0_1x0_0 | pad | bytes 16793602 | tf_op jit(solution)/shard_map/concatenate | solution.py:121
  501.7 11.6 %gather_fusion.1 = bf16[192,8192]{1,0:T(8,128)(2,1)} fusion(bf16[513,8192]{1,0:T(8,128)(2,1)} %concatenate.7, s32[1024]{0:T(1024)S(1)} %pad_clamp_fusion), kind=kCustom, calls=%fused_computation.1 | custom fusion | bytes 6292224 | tf_op jit(solution)/shard_map/jit(_take)/gather | solution.py:122
  513.2 3.9 broadcast_select_fusion.1
  (182 shorter events, 95.6 us)
Async XLA Ops:
  6.5 343.4 %copy-start = (bf16[256,2048]{1,0:T(8,128)(2,1)S(1)}, bf16[256,2048]{1,0:T(8,128)(2,1)}, u32[]{:S(2)}) copy-start(bf16[256,2048]{1,0:T(8,128)(2,1)} %param.8) | copy-start | bytes 3145732
  6.5 3.1 copy-start.5
  6.5 4.5 copy-start.4
  6.5 247.4 %all-gather.4.cloned.1.call-start = ((), (), s32[]{:S(2)}) async-start(), calls=%async_computation.2 | async-start | bytes 68157440 | tf_op jit(solution)/shard_map/all_gather | solution.py:12
  8.1 4.6 copy-start.3
  9.6 3.0 copy-start.1
  352.3 4.9 copy-start.2
  361.5 18.7 %all-to-all-start = ((bf16[4,64,2048]{2,1,0:T(8,128)(2,1)}), bf16[4,64,2048]{2,1,0:T(8,128)(2,1)S(1)}, u32[]{:S(2)}, u32[]{:S(2)}) async-start(bf16[4,64,2048]{2,1,0:T(8,128)(2,1)} %all_to_all.17), calls=%async_computation | async-start | bytes 2097152 | tf_op jit(solution)/shard_map/all_to_all | solution.py:90
  395.6 98.1 %all-to-all-start.1 = ((bf16[4,128,8192]{2,1,0:T(8,128)(2,1)}), bf16[4,128,8192]{2,1,0:T(8,128)(2,1)}, u32[]{:S(2)}, u32[]{:S(2)}) async-start(bf16[4,128,8192]{2,1,0:T(8,128)(2,1)} %broadcast_select_fusion), calls=%async_computation.1 | async-start | bytes 16777216 | tf_op jit(solution)/shard_map/all_to_all | solution.py:109
Sparse Core Ops, SparseCore 0:
  12.8 241.1 all-gather.3
where the time goes:
time: 527 us; the launch traced here: 524 us
  waiting for transfers between devices  209 us (40%)
  blocking collectives  130 us (25%)
  other arithmetic  110 us (21%)
  local copies, waits for them, and re-layouts  40.2 us (8%)
  between operations  14.3 us (3%)
  starting transfers between devices  9.84 us (2%)
  matrix products  8.68 us (2%)
    unnamed x1, blocking collectives  130 us
    all_gather x1, waiting for transfers between devices, entering(): everything = jax.tree.map(lambda part: lax.all_gather(part, axis), x)  107 us
    select_n x64, other arithmetic, hop(): return jax.tree.map(lambda a, b: jnp.where(reached, a, b), new, before)  93.3 us
    all_to_all x1, waiting for transfers between devices, on_device(): lax.all_to_all(outgoing, 'head', split_axis=0, concat_axis=0, tiled=True)  89.7 us
    all_to_all x1, waiting for transfers between devices, on_device(): lax.all_to_all(normed, 'head', split_axis=0, concat_axis=1, tiled=True)  12.2 us
    gather x1, local copies, waits for them, and re-layouts, on_device(): jnp.take(padded_in, recv_table, axis=0)  11.6 us
  transfers between devices with their start and end apart: 3, of which 3 were waited for; matrix products, arithmetic and copies ran while one was open for 2% of the time, Pallas kernels for 0%

commit v1 on v0

v1 whole, which is shorter than its diff:
```python
import functools

import jax
import jax.numpy as jnp
from jax import lax
from jax.experimental import pallas as pl
from jax.experimental.pallas import tpu as pltpu
from jax.sharding import PartitionSpec as P

EXPERTS = 32
CAP = 24
HD = 128
ROW = 16
GROUPS = 4
MESH = pl.DeviceIdType.MESH
F32 = jnp.float32
BF16 = jnp.bfloat16


def kernel(
    sizes,
    level_ref,
    routing_ref,
    gain_ref,
    q_hbm,
    k_hbm,
    v_hbm,
    out_ref,
    q_ref,
    k_ref,
    v_ref,
    state_ref,
    rows_ref,
    total_ref,
    back_ref,
    incoming_ref,
    intra_ref,
    pick_ref,
    picked_ref,
    block_decay_ref,
    row_decay_ref,
    load_sem,
    row_sem,
    total_sem,
    back_sem,
    out_sem,
):
    length, heads, seq_count, head_count = sizes
    across = seq_count // ROW
    per_group = heads // GROUPS
    width = per_group * HD
    piece = width // ROW
    features = heads * HD
    seats = EXPERTS // head_count * CAP

    seq = lax.axis_index("seq")
    me_head = lax.axis_index("head")
    me_row = lax.rem(seq, ROW)
    me_x = lax.div(seq, ROW)
    row_base = me_x * ROW

    loads = []
    for g in range(GROUPS):
        cols = pl.ds(g * width, width)
        loads.append([
            pltpu.make_async_copy(k_hbm.at[:, cols], k_ref.at[:, cols], load_sem.at[0, g]),
            pltpu.make_async_copy(v_hbm.at[:, cols], v_ref.at[:, cols], load_sem.at[1, g]),
        ])
    for pair in loads:
        for copy in pair:
            copy.start()
    q_load = pltpu.make_async_copy(q_hbm, q_ref, load_sem.at[2, 0])
    q_load.start()

    barrier = pltpu.get_barrier_semaphore()

    def greet(device):
        pl.semaphore_signal(barrier, inc=1, device_id=device, device_id_type=MESH)

    def row_peer(d):
        return lax.rem(me_row + d, ROW)

    def x_peer(d):
        return lax.rem(me_x + d, across)

    def head_peer(d):
        return lax.rem(me_head + d, head_count)

    @pl.loop(1, ROW)
    def _(d):
        greet((row_base + row_peer(d), me_head))

    for d in range(1, across):
        greet((x_peer(d) * ROW + me_row, me_head))
    for d in range(1, head_count):
        greet((seq, head_peer(d)))

    def rate_row(h, n):
        level = jnp.full((1, n), level_ref[h], jnp.int32)
        return jnp.exp2(level.astype(F32) - 2.0) / (length * seq_count)

    for h in range(heads):
        rate = rate_row(h, HD)
        block_decay_ref[h] = jnp.broadcast_to(jnp.exp(-rate * length), (8, HD))
        row_decay_ref[h] = jnp.broadcast_to(jnp.exp(-rate * (length * ROW)), (8, HD))

    place = lax.broadcasted_iota(jnp.int32, (length, HD), 0).astype(F32)

    def head_cols(h):
        return pl.ds(h * HD, HD)

    def state(h):
        g, at = divmod(h, per_group)
        decay_out = jnp.exp(-rate_row(h, HD) * (length - 1.0 - place))
        weighted = (k_ref[:, head_cols(h)].astype(F32) * decay_out).astype(BF16)
        made = lax.dot_general(
            weighted, v_ref[:, head_cols(h)], (((0,), (0,)), ((), ())), preferred_element_type=F32
        )
        state_ref[g, pl.ds(at * HD, HD), :] = made.astype(BF16)

    def at_piece(r):
        return pl.ds(pl.multiple_of(r * piece, piece), piece)

    def row_copy(g, to):
        return pltpu.make_async_remote_copy(
            src_ref=state_ref.at[g, at_piece(to), :],
            dst_ref=rows_ref.at[g, at_piece(me_row), :],
            send_sem=row_sem.at[0, g],
            recv_sem=row_sem.at[1, g],
            device_id=(row_base + to, me_head),
            device_id_type=MESH,
        )

    def send_row(g):
        @pl.loop(1, ROW)
        def _(d):
            row_copy(g, row_peer(d)).start()

        rows_ref[g, at_piece(me_row), :] = state_ref[g, at_piece(me_row), :]

    def wait_bytes(ref, sem):
        pltpu.make_async_copy(ref, ref, sem).wait()

    others = pl.ds(0, (ROW - 1) * piece)

    def decays(ref, g):
        return jnp.broadcast_to(ref[g * per_group + lax.div(me_row * piece, HD)][0:1], (piece, HD))

    def total_copy(g, to):
        return pltpu.make_async_remote_copy(
            src_ref=total_ref.at[g, me_x],
            dst_ref=total_ref.at[g, me_x],
            send_sem=total_sem.at[0, g],
            recv_sem=total_sem.at[1, g],
            device_id=(to * ROW + me_row, me_head),
            device_id_type=MESH,
        )

    def sum_row(g):
        wait_bytes(rows_ref.at[g, others], row_sem.at[1, g])
        decay = decays(block_decay_ref, g)
        carried = jnp.zeros((piece, HD), F32)
        for r in range(ROW):
            carried = decay * carried + rows_ref[g, pl.ds(r * piece, piece), :].astype(F32)
        total_ref[g, me_x] = carried
        for d in range(1, across):
            total_copy(g, x_peer(d)).start()

    def back_copy(g, to):
        return pltpu.make_async_remote_copy(
            src_ref=back_ref.at[g, at_piece(to), :],
            dst_ref=incoming_ref.at[g, at_piece(me_row), :],
            send_sem=back_sem.at[0, g],
            recv_sem=back_sem.at[1, g],
            device_id=(row_base + to, me_head),
            device_id_type=MESH,
        )

    def give_back(g):
        wait_bytes(total_ref.at[g, pl.ds(0, across - 1)], total_sem.at[1, g])
        over_row = decays(row_decay_ref, g)
        carried = jnp.zeros((piece, HD), F32)
        for x in range(across):
            carried = jnp.where(x < me_x, over_row * carried + total_ref[g, x], carried)
        decay = decays(block_decay_ref, g)
        for r in range(ROW):
            back_ref[g, pl.ds(r * piece, piece), :] = carried.astype(BF16)
            carried = decay * carried + rows_ref[g, pl.ds(r * piece, piece), :].astype(F32)

        @pl.loop(1, ROW)
        def _(d):
            back_copy(g, row_peer(d)).start()

        incoming_ref[g, at_piece(me_row), :] = back_ref[g, at_piece(me_row), :]

    def intra(h):
        rows = lax.broadcasted_iota(jnp.int32, (length, length), 0)
        offset = rows - lax.broadcasted_iota(jnp.int32, (length, length), 1)
        decay = jnp.exp(-rate_row(h, length) * jnp.maximum(offset, 0).astype(F32))
        scores = lax.dot_general(
            q_ref[:, head_cols(h)],
            k_ref[:, head_cols(h)],
            (((1,), (1,)), ((), ())),
            preferred_element_type=F32,
        )
        weights = jnp.where(offset >= 0, scores * decay, 0.0).astype(BF16)
        intra_ref[:, head_cols(h)] = jnp.dot(
            weights, v_ref[:, head_cols(h)], preferred_element_type=F32
        )

    def make_pick():
        expert = lax.broadcasted_iota(jnp.int32, (EXPERTS, length), 0)
        named = (routing_ref[0:1, :] == expert) | (routing_ref[1:2, :] == expert)
        named = jnp.where(named, 1.0, 0.0)
        earlier = lax.broadcasted_iota(jnp.int32, (length, length), 0)
        earlier = earlier < lax.broadcasted_iota(jnp.int32, (length, length), 1)
        before = jnp.dot(
            named.astype(BF16), jnp.where(earlier, 1.0, 0.0).astype(BF16), preferred_element_type=F32
        )
        slot = jnp.where(named > 0.5, before, -1.0)
        seat = lax.broadcasted_iota(jnp.int32, (EXPERTS, CAP, length), 1).astype(F32)
        chosen = jnp.where(slot[:, None, :] == seat, 1.0, 0.0)
        pick_ref[...] = chosen.reshape(EXPERTS * CAP, length).astype(BF16)

    def out_copy(g, d):
        return pltpu.make_async_remote_copy(
            src_ref=picked_ref.at[g, d - 1],
            dst_ref=out_ref.at[:, pl.ds(pl.multiple_of(me_head * features + g * width, width), width)],
            send_sem=out_sem.at[0, g],
            recv_sem=out_sem.at[1, g],
            device_id=(seq, head_peer(d)),
            device_id_type=MESH,
        )

    def finish(g):
        wait_bytes(incoming_ref.at[g, others], back_sem.at[1, g])
        parts = []
        for at in range(per_group):
            h = g * per_group + at
            decay_in = jnp.exp(-rate_row(h, HD) * (place + 1.0))
            inter = jnp.dot(
                q_ref[:, head_cols(h)],
                incoming_ref[g, pl.ds(at * HD, HD), :],
                preferred_element_type=F32,
            )
            attended = inter * decay_in + intra_ref[:, head_cols(h)]
            mean = jnp.sum(attended * attended, axis=-1, keepdims=True) * (1.0 / HD)
            normed = attended * lax.rsqrt(mean + 1e-05) * gain_ref[h : h + 1, :]
            parts.append(normed.astype(BF16))
        normed = jnp.concatenate(parts, axis=1)

        def picked(d):
            owner = pl.ds(pl.multiple_of(head_peer(d) * seats, seats), seats)
            return jnp.dot(pick_ref[owner, :], normed, preferred_element_type=F32).astype(BF16)

        for d in range(1, head_count):
            picked_ref[g, d - 1] = picked(d)
            out_copy(g, d).start()
        out_ref[:, pl.ds(pl.multiple_of(me_head * features + g * width, width), width)] = picked(0)

    for g in range(GROUPS):
        for copy in loads[g]:
            copy.wait()
        for at in range(per_group):
            state(g * per_group + at)
        if g == 0:
            pl.semaphore_wait(barrier, ROW - 1 + across - 1 + head_count - 1)
        send_row(g)
    make_pick()
    q_load.wait()

    def intra_group(g):
        for at in range(per_group):
            intra(g * per_group + at)

    intra_group(0)
    sum_row(0)
    intra_group(1)
    give_back(0)
    sum_row(1)
    intra_group(2)
    give_back(1)
    sum_row(2)
    intra_group(3)
    finish(0)
    give_back(2)
    sum_row(3)
    finish(1)
    give_back(3)
    finish(2)
    finish(3)

    for g in range(GROUPS):
        wait_bytes(state_ref.at[g, others], row_sem.at[0, g])
        wait_bytes(total_ref.at[g, pl.ds(0, across - 1)], total_sem.at[0, g])
        wait_bytes(back_ref.at[g, others], back_sem.at[0, g])
        wait_bytes(picked_ref.at[g], out_sem.at[0, g])
        wait_bytes(picked_ref.at[g], out_sem.at[1, g])


def on_device(query, key_rows, value_rows, head_norm_gain, decay_level, routing):
    length, features = query.shape
    heads = decay_level.shape[0]
    seq_count = lax.axis_size("seq")
    head_count = lax.axis_size("head")
    across = seq_count // ROW
    width = features // GROUPS
    piece = width // ROW
    seats = EXPERTS // head_count * CAP
    whole = pl.BlockSpec(memory_space=pltpu.VMEM)
    outside = pl.BlockSpec(memory_space=pltpu.HBM)
    dispatched = pl.pallas_call(
        functools.partial(kernel, (length, heads, seq_count, head_count)),
        out_shape=jax.ShapeDtypeStruct((seats, features * head_count), BF16),
        in_specs=[pl.BlockSpec(memory_space=pltpu.SMEM), whole, whole, outside, outside, outside],
        out_specs=whole,
        scratch_shapes=[
            pltpu.VMEM((length, features), BF16),
            pltpu.VMEM((length, features), BF16),
            pltpu.VMEM((length, features), BF16),
            pltpu.VMEM((GROUPS, width, HD), BF16),
            pltpu.VMEM((GROUPS, width, HD), BF16),
            pltpu.VMEM((GROUPS, across, piece, HD), F32),
            pltpu.VMEM((GROUPS, width, HD), BF16),
            pltpu.VMEM((GROUPS, width, HD), BF16),
            pltpu.VMEM((length, features), F32),
            pltpu.VMEM((EXPERTS * CAP, length), BF16),
            pltpu.VMEM((GROUPS, head_count - 1, seats, width), BF16),
            pltpu.VMEM((heads, 8, HD), F32),
            pltpu.VMEM((heads, 8, HD), F32),
            pltpu.SemaphoreType.DMA((3, GROUPS)),
            pltpu.SemaphoreType.DMA((2, GROUPS)),
            pltpu.SemaphoreType.DMA((2, GROUPS)),
            pltpu.SemaphoreType.DMA((2, GROUPS)),
            pltpu.SemaphoreType.DMA((2, GROUPS)),
        ],
        compiler_params=pltpu.CompilerParams(
            collective_id=0, has_side_effects=True, vmem_limit_bytes=40 << 20
        ),
        name="attend_and_dispatch",
    )(
        decay_level,
        routing.T,
        head_norm_gain.reshape(heads, HD),
        query,
        key_rows,
        value_rows,
    )
    return dispatched.reshape(EXPERTS // head_count, CAP, features * head_count)


def solution(mesh):
    in_specs = (
        P("seq", "head"),
        P("seq", "head"),
        P("seq", "head"),
        P("head"),
        P("head"),
        P("seq", None),
    )
    out_specs = P("head", "seq", None)
    return jax.shard_map(
        on_device, mesh=mesh, in_specs=in_specs, out_specs=out_specs, check_vma=False
    )
```

time: 527 us -> 73.1 us (0.14)
  waiting for transfers between devices: 209 us -> 0 us
  blocking collectives: 130 us -> 0 us
  other arithmetic: 110 us -> 0 us
  Pallas kernels: 0 us -> 65.5 us
  local copies, waits for them, and re-layouts: 40.2 us -> 7.37 us
  between operations: 14.3 us -> 0.02 us
  starting transfers between devices: 9.84 us -> 0 us
  matrix products: 8.68 us -> 0 us
    unnamed x1 -> x0, blocking collectives: 130 us -> none
    all_gather x1 -> x0, waiting for transfers between devices: 107 us -> none  [entering(): everything = jax.tree.map(lambda part: lax.all_gather(part, axis), x)]
    select_n x70 -> x0, other arithmetic: 105 us -> none  [the longest x64 93.3 us: hop(): return jax.tree.map(lambda a, b: jnp.where(reached, a, b), new, before)]
    all_to_all x2 -> x0, waiting for transfers between devices: 102 us -> none  [the longest x1 89.7 us: on_device(): lax.all_to_all(outgoing, 'head', split_axis=0, concat_axis=0, tiled=True)]
    pallas_call x0 -> x1, Pallas kernels: none -> 65.5 us  [on_device(): pl.pallas_call(functools.partial(kernel, (length, heads, seq_count, head_...]
    gather x2 -> x0, local copies, waits for them, and re-layouts: 19.4 us -> none  [the longest x1 11.6 us: on_device(): jnp.take(padded_in, recv_table, axis=0)]
    all_to_all x2 -> x0, starting transfers between devices: 9.84 us -> none  [the longest x1 5.84 us: on_device(): lax.all_to_all(outgoing, 'head', split_axis=0, concat_axis=0, tiled=True)]
    dot_general x3 -> x0, matrix products: 8.68 us -> none  [the longest x1 4.92 us: on_device(): jnp.einsum('hlm,mhe->lhe', weights, value_heads, preferred_element_type=j...]
  transfers between devices with their start and end apart: 3 -> 0, of which waited for: 3 -> 0; matrix products, arithmetic and copies ran while one was open for 2% -> 0% of each run, Pallas kernels for 0% -> 0%
where the time goes in v1:
time: 73.1 us; the launch traced here: 72.9 us
  Pallas kernels  65.5 us (90%)
  local copies, waits for them, and re-layouts  7.37 us (10%)
    pallas_call x1, Pallas kernels, on_device(): pl.pallas_call(functools.partial(kernel, (length, heads, seq_count, head_...  65.5 us
    unnamed x13, local copies, waits for them, and re-layouts  7.37 us

profile of v1, /device:TPU:1, one launch (start us, length us, event | category | flops | bytes accessed | tf_op | source)
XLA Modules:
  0.0 72.9 jit_solution(1595296459361895882)
XLA Ops:
  0.0 0.0 copy-start
  0.0 1.2 %copy-done = bf16[256,2048]{1,0:T(8,128)(2,1)S(1)} copy-done((bf16[256,2048]{1,0:T(8,128)(2,1)S(1)}, bf16[256,2048]{1,0:T(8,128)(2,1)}, u32[]{:S(2)}) %copy-start) | copy-done | bytes 1048600
  1.2 0.0 copy-start.1
  1.2 1.2 %copy-done.1 = bf16[256,2048]{1,0:T(8,128)(2,1)S(1)} copy-done((bf16[256,2048]{1,0:T(8,128)(2,1)S(1)}, bf16[256,2048]{1,0:T(8,128)(2,1)}, u32[]{:S(2)}) %copy-start.1) | copy-done | bytes 1048600
  2.5 0.0 copy-start.2
  2.5 1.2 %copy-done.2 = bf16[256,2048]{1,0:T(8,128)(2,1)S(1)} copy-done((bf16[256,2048]{1,0:T(8,128)(2,1)S(1)}, bf16[256,2048]{1,0:T(8,128)(2,1)}, u32[]{:S(2)}) %copy-start.2) | copy-done | bytes 1048600
  3.7 0.0 copy-start.3
  3.7 0.7 copy-done.3
  4.4 0.0 copy-start.4
  4.4 0.7 copy-done.4
  5.1 0.0 copy-start.5
  5.1 0.7 copy-done.5
  5.7 65.5 %attend_and_dispatch.1 = bf16[192,8192]{1,0:T(8,128)(2,1)S(1)} custom-call(s32[16]{0:T(128)S(1)} %copy-done.5, s32[2,256]{1,0:T(2,128)S(1)} %bitcast.5, f32[16,128]{1,0:T(8,128)S(1)} %bitcast.4, bf16[256,2048]{1,0:T(8,128)(2,1)S(1)} %copy-done, bf16[256,2048]{1,0:T(8,128)(2,1)S(1)} %copy-done.1, bf16[256,2048]{1,0:T(8,128)(2,1)S(1)} %copy-done.2), custom_call_target="tpu_custom_call" | custom-call | tf_op jit(solution)/shard_map/attend_and_dispatch/pallas_call | solution.py:312
  71.2 1.7 %copy.8 = bf16[8,24,8192]{2,1,0:T(8,128)(2,1)} copy(bf16[8,24,8192]{2,1,0:T(8,128)(2,1)S(1)} %bitcast.3) | data formatting | bytes 6291456
Async XLA Ops:
  0.0 1.2 %copy-start = (bf16[256,2048]{1,0:T(8,128)(2,1)S(1)}, bf16[256,2048]{1,0:T(8,128)(2,1)}, u32[]{:S(2)}) copy-start(bf16[256,2048]{1,0:T(8,128)(2,1)} %q_hbm.1) | copy-start | bytes 3145732
  1.2 1.2 %copy-start.1 = (bf16[256,2048]{1,0:T(8,128)(2,1)S(1)}, bf16[256,2048]{1,0:T(8,128)(2,1)}, u32[]{:S(2)}) copy-start(bf16[256,2048]{1,0:T(8,128)(2,1)} %k_hbm.1) | copy-start | bytes 3145732
  2.5 1.2 %copy-start.2 = (bf16[256,2048]{1,0:T(8,128)(2,1)S(1)}, bf16[256,2048]{1,0:T(8,128)(2,1)}, u32[]{:S(2)}) copy-start(bf16[256,2048]{1,0:T(8,128)(2,1)} %v_hbm.1) | copy-start | bytes 3145732
  3.7 0.7 copy-start.3
  4.4 0.7 copy-start.4
  5.1 0.7 copy-start.5

commit v2 on v1

v2 whole, which is shorter than its diff:
```python
import functools

import jax
import jax.numpy as jnp
from jax import lax
from jax.experimental import pallas as pl
from jax.experimental.pallas import tpu as pltpu
from jax.sharding import PartitionSpec as P

EXPERTS = 32
CAP = 24
HD = 128
ROW = 16
SIZES = (2, 2, 4, 4, 4)
GROUPS = len(SIZES)
FIRST = tuple(sum(SIZES[:g]) for g in range(GROUPS))
MESH = pl.DeviceIdType.MESH
F32 = jnp.float32
BF16 = jnp.bfloat16


def kernel(
    sizes,
    level_hbm,
    routing_hbm,
    gain_hbm,
    q_hbm,
    k_hbm,
    v_hbm,
    out_ref,
    level_ref,
    routing_ref,
    gain_ref,
    q_ref,
    k_ref,
    v_ref,
    state_ref,
    rows_ref,
    total_ref,
    back_ref,
    incoming_ref,
    intra_ref,
    normed_ref,
    landed_ref,
    pick_ref,
    picked_ref,
    block_decay_ref,
    row_decay_ref,
    small_sem,
    load_sem,
    row_sem,
    total_sem,
    back_sem,
    landed_sem,
    sent_sem,
    out_sem,
):
    length, heads, seq_count, head_count = sizes
    across = seq_count // ROW
    features = heads * HD
    seats = EXPERTS // head_count * CAP

    seq = lax.axis_index("seq")
    me_head = lax.axis_index("head")
    me_row = lax.rem(seq, ROW)
    me_x = lax.div(seq, ROW)
    row_base = me_x * ROW
    up = lax.rem(me_head + 1, head_count)
    down = lax.rem(me_head + head_count - 1, head_count)

    level_load = pltpu.make_async_copy(level_hbm, level_ref, small_sem.at[0])
    level_load.start()
    loads = []
    for g in range(GROUPS):
        cols = pl.ds(FIRST[g] * HD, SIZES[g] * HD)
        pair = [
            pltpu.make_async_copy(k_hbm.at[:, cols], k_ref.at[:, cols], load_sem.at[0, g]),
            pltpu.make_async_copy(v_hbm.at[:, cols], v_ref.at[:, cols], load_sem.at[1, g]),
        ]
        for copy in pair:
            copy.start()
        loads.append(pair)
    routing_load = pltpu.make_async_copy(routing_hbm, routing_ref, small_sem.at[1])
    routing_load.start()
    q_load = pltpu.make_async_copy(q_hbm, q_ref, small_sem.at[2])
    q_load.start()
    gain_load = pltpu.make_async_copy(gain_hbm, gain_ref, small_sem.at[3])
    gain_load.start()

    barrier = pltpu.get_barrier_semaphore()

    def greet(device):
        pl.semaphore_signal(barrier, inc=1, device_id=device, device_id_type=MESH)

    def row_peer(d):
        return lax.rem(me_row + d, ROW)

    def x_peer(d):
        return lax.rem(me_x + d, across)

    @pl.loop(1, ROW)
    def _(d):
        greet((row_base + row_peer(d), me_head))

    for d in range(1, across):
        greet((x_peer(d) * ROW + me_row, me_head))
    greet((seq, up))
    greet((seq, down))

    def rate_row(h, n):
        level = jnp.full((1, n), level_ref[h], jnp.int32)
        return jnp.exp2(level.astype(F32) - 2.0) / (length * seq_count)

    place = lax.broadcasted_iota(jnp.int32, (length, HD), 0).astype(F32)

    def head_cols(h):
        return pl.ds(h * HD, HD)

    def state(h):
        decay_out = jnp.exp(-rate_row(h, HD) * (length - 1.0 - place))
        weighted = (k_ref[:, head_cols(h)].astype(F32) * decay_out).astype(BF16)
        made = lax.dot_general(
            weighted, v_ref[:, head_cols(h)], (((0,), (0,)), ((), ())), preferred_element_type=F32
        )
        state_ref[pl.ds(h * HD, HD), :] = made.astype(BF16)

    def piece_of(g):
        return SIZES[g] * HD // ROW

    def at_piece(g, r):
        rows = piece_of(g)
        return pl.ds(pl.multiple_of(FIRST[g] * HD + r * rows, rows), rows)

    def others(g):
        return pl.ds(FIRST[g] * HD, (ROW - 1) * piece_of(g))

    def wait_bytes(ref, sem):
        pltpu.make_async_copy(ref, ref, sem).wait()

    def row_copy(g, to):
        return pltpu.make_async_remote_copy(
            src_ref=state_ref.at[at_piece(g, to), :],
            dst_ref=rows_ref.at[at_piece(g, me_row), :],
            send_sem=row_sem.at[0, g],
            recv_sem=row_sem.at[1, g],
            device_id=(row_base + to, me_head),
            device_id_type=MESH,
        )

    def send_row(g):
        @pl.loop(1, ROW)
        def _(d):
            row_copy(g, row_peer(d)).start()

        rows_ref[at_piece(g, me_row), :] = state_ref[at_piece(g, me_row), :]

    def decays(ref, g):
        mine = FIRST[g] + lax.div(me_row * piece_of(g), HD)
        return jnp.broadcast_to(ref[mine][0:1], (piece_of(g), HD))

    def at_total(g):
        return pl.ds(FIRST[g] * HD // ROW, piece_of(g))

    def total_copy(g, to):
        return pltpu.make_async_remote_copy(
            src_ref=total_ref.at[me_x, at_total(g)],
            dst_ref=total_ref.at[me_x, at_total(g)],
            send_sem=total_sem.at[0, g],
            recv_sem=total_sem.at[1, g],
            device_id=(to * ROW + me_row, me_head),
            device_id_type=MESH,
        )

    def member(g, r):
        return pl.ds(FIRST[g] * HD + r * piece_of(g), piece_of(g))

    def sum_row(g):
        wait_bytes(rows_ref.at[others(g)], row_sem.at[1, g])
        decay = decays(block_decay_ref, g)
        carried = rows_ref[member(g, 0), :].astype(F32)
        for r in range(1, ROW):
            carried = decay * carried + rows_ref[member(g, r), :].astype(F32)
        total_ref[me_x, at_total(g)] = carried
        for d in range(1, across):
            total_copy(g, x_peer(d)).start()

    def back_copy(g, to):
        return pltpu.make_async_remote_copy(
            src_ref=back_ref.at[at_piece(g, to), :],
            dst_ref=incoming_ref.at[at_piece(g, me_row), :],
            send_sem=back_sem.at[0, g],
            recv_sem=back_sem.at[1, g],
            device_id=(row_base + to, me_head),
            device_id_type=MESH,
        )

    def give_back(g):
        wait_bytes(total_ref.at[pl.ds(0, across - 1), at_total(g)], total_sem.at[1, g])
        over_row = decays(row_decay_ref, g)
        carried = jnp.zeros((piece_of(g), HD), F32)
        for x in range(across):
            carried = jnp.where(x < me_x, over_row * carried + total_ref[x, at_total(g)], carried)
        decay = decays(block_decay_ref, g)
        for r in range(ROW):
            back_ref[member(g, r), :] = carried.astype(BF16)
            carried = decay * carried + rows_ref[member(g, r), :].astype(F32)

        @pl.loop(1, ROW)
        def _(d):
            back_copy(g, row_peer(d)).start()

        incoming_ref[at_piece(g, me_row), :] = back_ref[at_piece(g, me_row), :]

    def intra(h):
        rows = lax.broadcasted_iota(jnp.int32, (length, length), 0)
        offset = rows - lax.broadcasted_iota(jnp.int32, (length, length), 1)
        decay = jnp.exp(-rate_row(h, length) * jnp.maximum(offset, 0).astype(F32))
        scores = lax.dot_general(
            q_ref[:, head_cols(h)],
            k_ref[:, head_cols(h)],
            (((1,), (1,)), ((), ())),
            preferred_element_type=F32,
        )
        weights = jnp.where(offset >= 0, scores * decay, 0.0).astype(BF16)
        intra_ref[:, head_cols(h)] = jnp.dot(
            weights, v_ref[:, head_cols(h)], preferred_element_type=F32
        )

    def make_pick():
        routing_load.wait()
        expert = lax.broadcasted_iota(jnp.int32, (EXPERTS, length), 0)
        named = (routing_ref[0:1, :] == expert) | (routing_ref[1:2, :] == expert)
        named = jnp.where(named, 1.0, 0.0)
        earlier = lax.broadcasted_iota(jnp.int32, (length, length), 0)
        earlier = earlier < lax.broadcasted_iota(jnp.int32, (length, length), 1)
        before = jnp.dot(
            named.astype(BF16), jnp.where(earlier, 1.0, 0.0).astype(BF16), preferred_element_type=F32
        )
        slot = jnp.where(named > 0.5, before, -1.0)
        seat = lax.broadcasted_iota(jnp.int32, (EXPERTS, CAP, length), 1).astype(F32)
        chosen = jnp.where(slot[:, None, :] == seat, 1.0, 0.0)
        pick_ref[...] = chosen.reshape(EXPERTS * CAP, length).astype(BF16)

    def half_cols(g, half):
        return pl.ds((FIRST[g] + half * SIZES[g] // 2) * HD, SIZES[g] // 2 * HD)

    def packed_cols(g):
        return pl.ds(FIRST[g] // 2 * HD, SIZES[g] // 2 * HD)

    def out_cols(g, half, head):
        first = (FIRST[g] + half * SIZES[g] // 2) * HD
        return pl.ds(pl.multiple_of(head * features + first, HD), SIZES[g] // 2 * HD)

    def picked_rows(owner, block):
        rows = pl.ds(pl.multiple_of(owner * seats, seats), seats)
        return jnp.dot(pick_ref[rows, :], block, preferred_element_type=F32).astype(BF16)

    def whole_copy(g, half):
        return pltpu.make_async_remote_copy(
            src_ref=normed_ref.at[:, half_cols(g, half)],
            dst_ref=landed_ref.at[half, :, packed_cols(g)],
            send_sem=sent_sem.at[0],
            recv_sem=landed_sem.at[half, g],
            device_id=(seq, down if half else up),
            device_id_type=MESH,
        )

    def send_picked(g, half, origin, place_at, to):
        pltpu.make_async_remote_copy(
            src_ref=picked_ref.at[place_at, :, packed_cols(g)],
            dst_ref=out_ref.at[:, out_cols(g, half, origin)],
            send_sem=sent_sem.at[1],
            recv_sem=out_sem.at[0],
            device_id=(seq, to),
            device_id_type=MESH,
        ).start()

    def finish(g):
        wait_bytes(incoming_ref.at[others(g)], back_sem.at[1, g])
        for half in range(2):
            for at in range(SIZES[g] // 2):
                h = FIRST[g] + half * SIZES[g] // 2 + at
                decay_in = jnp.exp(-rate_row(h, HD) * (place + 1.0))
                inter = jnp.dot(
                    q_ref[:, head_cols(h)],
                    incoming_ref[pl.ds(h * HD, HD), :],
                    preferred_element_type=F32,
                )
                attended = inter * decay_in + intra_ref[:, head_cols(h)]
                mean = jnp.sum(attended * attended, axis=-1, keepdims=True) * (1.0 / HD)
                normed = attended * lax.rsqrt(mean + 1e-05) * gain_ref[h : h + 1, :]
                normed_ref[:, head_cols(h)] = normed.astype(BF16)
            whole_copy(g, half).start()
        for half, to in ((1, up), (0, down)):
            picked_ref[half, :, packed_cols(g)] = picked_rows(to, normed_ref[:, half_cols(g, half)])
            send_picked(g, half, me_head, half, to)
        for half in range(2):
            out_ref[:, out_cols(g, half, me_head)] = picked_rows(
                me_head, normed_ref[:, half_cols(g, half)]
            )

    def relay(g):
        for half, origin, to in ((0, down, up), (1, up, down)):
            whole_copy(g, half).wait_recv()
            block = landed_ref[half, :, packed_cols(g)]
            picked_ref[2 + half, :, packed_cols(g)] = picked_rows(to, block)
            send_picked(g, half, origin, 2 + half, to)
        for half, origin in ((0, down), (1, up)):
            out_ref[:, out_cols(g, half, origin)] = picked_rows(
                me_head, landed_ref[half, :, packed_cols(g)]
            )

    level_load.wait()
    for g in range(GROUPS):
        for copy in loads[g]:
            copy.wait()
        for at in range(SIZES[g]):
            state(FIRST[g] + at)
        if g == 0:
            pl.semaphore_wait(barrier, ROW - 1 + across - 1 + 2)
        send_row(g)
    for h in range(heads):
        rate = rate_row(h, HD)
        block_decay_ref[h] = jnp.broadcast_to(jnp.exp(-rate * length), (8, HD))
        row_decay_ref[h] = jnp.broadcast_to(jnp.exp(-rate * (length * ROW)), (8, HD))
    make_pick()
    q_load.wait()
    gain_load.wait()

    def intra_group(g):
        for at in range(SIZES[g]):
            intra(FIRST[g] + at)

    sum_row(0)
    intra_group(0)
    sum_row(1)
    intra_group(1)
    intra_group(2)
    give_back(0)
    sum_row(2)
    give_back(1)
    sum_row(3)
    intra_group(3)
    give_back(2)
    finish(0)
    sum_row(4)
    finish(1)
    give_back(3)
    intra_group(4)
    relay(0)
    relay(1)
    finish(2)
    give_back(4)
    finish(3)
    relay(2)
    finish(4)
    relay(3)
    relay(4)

    for g in range(GROUPS):
        wait_bytes(state_ref.at[others(g)], row_sem.at[0, g])
        wait_bytes(total_ref.at[pl.ds(0, across - 1), at_total(g)], total_sem.at[0, g])
        wait_bytes(back_ref.at[others(g)], back_sem.at[0, g])
    wait_bytes(normed_ref, sent_sem.at[0])
    wait_bytes(picked_ref, sent_sem.at[1])
    wait_bytes(out_ref.at[:, pl.ds(0, 2 * features)], out_sem.at[0])


def on_device(query, key_rows, value_rows, head_norm_gain, decay_level, routing):
    length, features = query.shape
    heads = decay_level.shape[0]
    seq_count = lax.axis_size("seq")
    head_count = lax.axis_size("head")
    across = seq_count // ROW
    seats = EXPERTS // head_count * CAP
    outside = pl.BlockSpec(memory_space=pltpu.HBM)
    operands = [
        decay_level,
        routing.T,
        head_norm_gain.reshape(heads, HD),
        query,
        key_rows,
        value_rows,
    ]
    dispatched = pl.pallas_call(
        functools.partial(kernel, (length, heads, seq_count, head_count)),
        out_shape=jax.ShapeDtypeStruct((seats, features * head_count), BF16),
        in_specs=[outside] * len(operands),
        out_specs=pl.BlockSpec(memory_space=pltpu.VMEM),
        scratch_shapes=[
            pltpu.SMEM((heads,), jnp.int32),
            pltpu.VMEM((2, length), jnp.int32),
            pltpu.VMEM((heads, HD), F32),
            pltpu.VMEM((length, features), BF16),
            pltpu.VMEM((length, features), BF16),
            pltpu.VMEM((length, features), BF16),
            pltpu.VMEM((features, HD), BF16),
            pltpu.VMEM((features, HD), BF16),
            pltpu.VMEM((across, features // ROW, HD), F32),
            pltpu.VMEM((features, HD), BF16),
            pltpu.VMEM((features, HD), BF16),
            pltpu.VMEM((length, features), F32),
            pltpu.VMEM((length, features), BF16),
            pltpu.VMEM((2, length, features // 2), BF16),
            pltpu.VMEM((EXPERTS * CAP, length), BF16),
            pltpu.VMEM((4, seats, features // 2), BF16),
            pltpu.VMEM((heads, 8, HD), F32),
            pltpu.VMEM((heads, 8, HD), F32),
            pltpu.SemaphoreType.DMA((4,)),
            pltpu.SemaphoreType.DMA((2, GROUPS)),
            pltpu.SemaphoreType.DMA((2, GROUPS)),
            pltpu.SemaphoreType.DMA((2, GROUPS)),
            pltpu.SemaphoreType.DMA((2, GROUPS)),
            pltpu.SemaphoreType.DMA((2, GROUPS)),
            pltpu.SemaphoreType.DMA((2,)),
            pltpu.SemaphoreType.DMA((1,)),
        ],
        compiler_params=pltpu.CompilerParams(
            collective_id=0, has_side_effects=True, vmem_limit_bytes=40 << 20
        ),
        name="attend_and_dispatch",
    )(*[pltpu.with_memory_space_constraint(x, pltpu.HBM) for x in operands])
    return dispatched.reshape(EXPERTS // head_count, CAP, features * head_count)


def solution(mesh):
    in_specs = (
        P("seq", "head"),
        P("seq", "head"),
        P("seq", "head"),
        P("head"),
        P("head"),
        P("seq", None),
    )
    out_specs = P("head", "seq", None)
    return jax.shard_map(
        on_device, mesh=mesh, in_specs=in_specs, out_specs=out_specs, check_vma=False
    )
```

time: 73.1 us -> 58.1 us (0.79)
  Pallas kernels: 65.5 us -> 56.3 us
  local copies, waits for them, and re-layouts: 7.37 us -> 1.67 us
    pallas_call x1, Pallas kernels: 65.5 us -> 56.3 us  [on_device(): pl.pallas_call(functools.partial(kernel, (length, heads, seq_count, head_...]
    unnamed x13 -> x1, local copies, waits for them, and re-layouts: 7.37 us -> 1.67 us
where the time goes in v2:
time: 58.1 us; the launch traced here: 58 us
  Pallas kernels  56.3 us (97%)
  local copies, waits for them, and re-layouts  1.67 us (3%)
    pallas_call x1, Pallas kernels, on_device(): pl.pallas_call(functools.partial(kernel, (length, heads, seq_count, head_...  56.3 us
    unnamed x1, local copies, waits for them, and re-layouts  1.67 us

profile of v2, /device:TPU:1, one launch (start us, length us, event | category | flops | bytes accessed | tf_op | source)
XLA Modules:
  0.0 58.0 jit_solution(9934235104095373947)
XLA Ops:
  0.0 56.3 %attend_and_dispatch.1 = bf16[192,8192]{1,0:T(8,128)(2,1)S(1)} custom-call(s32[16]{0:T(128)} %level_hbm.1, s32[2,256]{1,0:T(2,128)} %bitcast.5, f32[16,128]{1,0:T(8,128)} %bitcast.4, bf16[256,2048]{1,0:T(8,128)(2,1)} %q_hbm.1, bf16[256,2048]{1,0:T(8,128)(2,1)} %k_hbm.1, bf16[256,2048]{1,0:T(8,128)(2,1)} %v_hbm.1), custom_call_target="tpu_custom_call" | custom-call | tf_op jit(solution)/shard_map/attend_and_dispatch/pallas_call | solution.py:385
  56.3 1.7 %copy.8 = bf16[8,24,8192]{2,1,0:T(8,128)(2,1)} copy(bf16[8,24,8192]{2,1,0:T(8,128)(2,1)S(1)} %bitcast.3) | data formatting | bytes 6291456

commit v3 on v2

--- a/solution.py
+++ b/solution.py
@@ -95,6 +95,9 @@
     def row_peer(d):
         return lax.rem(me_row + d, ROW)
 
+    def far_first(i):
+        return ROW // 2 + lax.div(i + 1, 2) * (1 - 2 * lax.rem(i, 2))
+
     def x_peer(d):
         return lax.rem(me_x + d, across)
 
@@ -148,9 +151,9 @@
         )
 
     def send_row(g):
-        @pl.loop(1, ROW)
-        def _(d):
-            row_copy(g, row_peer(d)).start()
+        @pl.loop(0, ROW - 1)
+        def _(i):
+            row_copy(g, row_peer(far_first(i))).start()
 
         rows_ref[at_piece(g, me_row), :] = state_ref[at_piece(g, me_row), :]
 
@@ -205,9 +208,9 @@
             back_ref[member(g, r), :] = carried.astype(BF16)
             carried = decay * carried + rows_ref[member(g, r), :].astype(F32)
 
-        @pl.loop(1, ROW)
-        def _(d):
-            back_copy(g, row_peer(d)).start()
+        @pl.loop(0, ROW - 1)
+        def _(i):
+            back_copy(g, row_peer(far_first(i))).start()
 
         incoming_ref[at_piece(g, me_row), :] = back_ref[at_piece(g, me_row), :]
 
@@ -310,15 +313,26 @@
                 me_head, landed_ref[half, :, packed_cols(g)]
             )
 
-    level_load.wait()
-    for g in range(GROUPS):
+    def intra_group(g):
+        for at in range(SIZES[g]):
+            intra(FIRST[g] + at)
+
+    def states(g):
         for copy in loads[g]:
             copy.wait()
         for at in range(SIZES[g]):
             state(FIRST[g] + at)
-        if g == 0:
-            pl.semaphore_wait(barrier, ROW - 1 + across - 1 + 2)
-        send_row(g)
+
+    level_load.wait()
+    states(0)
+    pl.semaphore_wait(barrier, ROW - 1 + across - 1 + 2)
+    send_row(0)
+    states(1)
+    send_row(1)
+    states(2)
+    send_row(2)
+    states(3)
+    send_row(3)
     for h in range(heads):
         rate = rate_row(h, HD)
         block_decay_ref[h] = jnp.broadcast_to(jnp.exp(-rate * length), (8, HD))
@@ -326,29 +340,26 @@
     make_pick()
     q_load.wait()
     gain_load.wait()
-
-    def intra_group(g):
-        for at in range(SIZES[g]):
-            intra(FIRST[g] + at)
-
+    states(4)
+    intra_group(0)
     sum_row(0)
-    intra_group(0)
+    intra_group(1)
     sum_row(1)
-    intra_group(1)
     intra_group(2)
     give_back(0)
+    give_back(1)
+    send_row(4)
     sum_row(2)
-    give_back(1)
     sum_row(3)
     intra_group(3)
     give_back(2)
     finish(0)
-    sum_row(4)
     finish(1)
     give_back(3)
-    intra_group(4)
     relay(0)
     relay(1)
+    sum_row(4)
+    intra_group(4)
     finish(2)
     give_back(4)
     finish(3)

time: 58.1 us -> 56.4 us (0.971)
  Pallas kernels: 56.3 us -> 54.6 us
    pallas_call x1, Pallas kernels: 56.3 us -> 54.6 us  [on_device(): pl.pallas_call(functools.partial(kernel, (length, heads, seq_count, head_...]
where the time goes in v3:
time: 56.4 us; the launch traced here: 56.3 us
  Pallas kernels  54.6 us (97%)
  local copies, waits for them, and re-layouts  1.67 us (3%)
    pallas_call x1, Pallas kernels, on_device(): pl.pallas_call(functools.partial(kernel, (length, heads, seq_count, head_...  54.6 us
    unnamed x1, local copies, waits for them, and re-layouts  1.67 us

profile of v3, /device:TPU:1, one launch (start us, length us, event | category | flops | bytes accessed | tf_op | source)
XLA Modules:
  0.0 56.3 jit_solution(679812607665642658)
XLA Ops:
  0.0 54.6 %attend_and_dispatch.1 = bf16[192,8192]{1,0:T(8,128)(2,1)S(1)} custom-call(s32[16]{0:T(128)} %level_hbm.1, s32[2,256]{1,0:T(2,128)} %bitcast.5, f32[16,128]{1,0:T(8,128)} %bitcast.4, bf16[256,2048]{1,0:T(8,128)(2,1)} %q_hbm.1, bf16[256,2048]{1,0:T(8,128)(2,1)} %k_hbm.1, bf16[256,2048]{1,0:T(8,128)(2,1)} %v_hbm.1), custom_call_target="tpu_custom_call" | custom-call | tf_op jit(solution)/shard_map/attend_and_dispatch/pallas_call | solution.py:396
  54.6 1.7 %copy.8 = bf16[8,24,8192]{2,1,0:T(8,128)(2,1)} copy(bf16[8,24,8192]{2,1,0:T(8,128)(2,1)S(1)} %bitcast.3) | data formatting | bytes 6291456

commit v4 on v3

--- a/solution.py
+++ b/solution.py
@@ -13,6 +13,7 @@
 ROW = 16
 SIZES = (2, 2, 4, 4, 4)
 GROUPS = len(SIZES)
+LENT = 2
 FIRST = tuple(sum(SIZES[:g]) for g in range(GROUPS))
 MESH = pl.DeviceIdType.MESH
 F32 = jnp.float32
@@ -44,6 +45,12 @@
     landed_ref,
     pick_ref,
     picked_ref,
+    lent_ref,
+    lent_landed_ref,
+    lent_picked_ref,
+    lent_rows_ref,
+    lent_state_ref,
+    lent_gain_ref,
     block_decay_ref,
     row_decay_ref,
     small_sem,
@@ -54,6 +61,11 @@
     landed_sem,
     sent_sem,
     out_sem,
+    lent_landed_sem,
+    lent_sent_sem,
+    lent_rows_sem,
+    lent_state_sem,
+    lent_gain_sem,
 ):
     length, heads, seq_count, head_count = sizes
     across = seq_count // ROW
@@ -67,6 +79,9 @@
     row_base = me_x * ROW
     up = lax.rem(me_head + 1, head_count)
     down = lax.rem(me_head + head_count - 1, head_count)
+    far = lax.rem(me_head + 2, head_count)
+    lent_width = SIZES[LENT] * HD
+    lent_half = lent_width // 2
 
     level_load = pltpu.make_async_copy(level_hbm, level_ref, small_sem.at[0])
     level_load.start()
@@ -109,6 +124,7 @@
         greet((x_peer(d) * ROW + me_row, me_head))
     greet((seq, up))
     greet((seq, down))
+    greet((seq, far))
 
     def rate_row(h, n):
         level = jnp.full((1, n), level_ref[h], jnp.int32)
@@ -280,6 +296,9 @@
 
     def finish(g):
         wait_bytes(incoming_ref.at[others(g)], back_sem.at[1, g])
+        if g == LENT:
+            for to, way in ((up, 0), (down, 1)):
+                state_copy(to, way).start()
         for half in range(2):
             for at in range(SIZES[g] // 2):
                 h = FIRST[g] + half * SIZES[g] // 2 + at
@@ -293,8 +312,9 @@
                 mean = jnp.sum(attended * attended, axis=-1, keepdims=True) * (1.0 / HD)
                 normed = attended * lax.rsqrt(mean + 1e-05) * gain_ref[h : h + 1, :]
                 normed_ref[:, head_cols(h)] = normed.astype(BF16)
-            whole_copy(g, half).start()
-        for half, to in ((1, up), (0, down)):
+            if g != LENT:
+                whole_copy(g, half).start()
+        for half, to in () if g == LENT else ((1, up), (0, down)):
             picked_ref[half, :, packed_cols(g)] = picked_rows(to, normed_ref[:, half_cols(g, half)])
             send_picked(g, half, me_head, half, to)
         for half in range(2):
@@ -313,68 +333,205 @@
                 me_head, landed_ref[half, :, packed_cols(g)]
             )
 
+    def lent_cols(half):
+        return pl.ds(half * lent_half, lent_half)
+
+    def lent_whole_copy(part, half):
+        return pltpu.make_async_remote_copy(
+            src_ref=lent_ref.at[part, :, lent_cols(half)],
+            dst_ref=lent_landed_ref.at[part, half],
+            send_sem=lent_sent_sem.at[0],
+            recv_sem=lent_landed_sem.at[part, half],
+            device_id=(seq, down if half else up),
+            device_id_type=MESH,
+        )
+
+    def send_lent(part, half, origin, place_at, to):
+        pltpu.make_async_remote_copy(
+            src_ref=lent_picked_ref.at[part, place_at],
+            dst_ref=lent_rows_ref.at[part, origin, :, lent_cols(half)],
+            send_sem=lent_sent_sem.at[1],
+            recv_sem=lent_rows_sem.at[0],
+            device_id=(seq, to),
+            device_id_type=MESH,
+        ).start()
+
+    def lend(part):
+        for half in range(2):
+            for at in range(SIZES[LENT] // 2):
+                at = half * SIZES[LENT] // 2 + at
+                h = FIRST[LENT] + at
+                if part == 0:
+                    decay_in = jnp.exp(-rate_row(h, HD) * (place + 1.0))
+                    value = q_ref[:, head_cols(h)].astype(F32) * decay_in
+                else:
+                    value = intra_ref[:, head_cols(h)]
+                lent_ref[part, :, head_cols(at)] = value.astype(BF16)
+            lent_whole_copy(part, half).start()
+
+    def lend_picked(part):
+        for half, to in ((1, up), (0, down)):
+            lent_picked_ref[part, half] = picked_rows(to, lent_ref[part, :, lent_cols(half)])
+            send_lent(part, half, me_head, half, to)
+
+    def lend_on(part):
+        for half, origin, to in ((0, down, up), (1, up, down)):
+            lent_whole_copy(part, half).wait_recv()
+            block = lent_landed_ref[part, half]
+            lent_picked_ref[part, 2 + half] = picked_rows(to, block)
+            send_lent(part, half, origin, 2 + half, to)
+        for half, origin in ((0, down), (1, up)):
+            lent_rows_ref[part, origin, :, lent_cols(half)] = picked_rows(
+                me_head, lent_landed_ref[part, half]
+            )
+
+    def gain_copy(to):
+        return pltpu.make_async_remote_copy(
+            src_ref=lent_gain_ref.at[me_head],
+            dst_ref=lent_gain_ref.at[me_head],
+            send_sem=lent_gain_sem.at[0],
+            recv_sem=lent_gain_sem.at[1],
+            device_id=(seq, to),
+            device_id_type=MESH,
+        )
+
+    def lend_gain():
+        lent_gain_ref[me_head, pl.ds(0, SIZES[LENT]), :] = gain_ref[pl.ds(FIRST[LENT], SIZES[LENT]), :]
+        for to in (up, down, far):
+            gain_copy(to).start()
+
+    def state_copy(to, way):
+        return pltpu.make_async_remote_copy(
+            src_ref=incoming_ref.at[pl.ds(FIRST[LENT] * HD, lent_width)],
+            dst_ref=lent_state_ref.at[me_head],
+            send_sem=lent_sent_sem.at[2],
+            recv_sem=lent_state_sem.at[way],
+            device_id=(seq, to),
+            device_id_type=MESH,
+        )
+
+    def lend_states_on():
+        for half, origin, to in ((0, down, up), (1, up, down)):
+            state_copy(to, half).wait_recv()
+            pltpu.make_async_remote_copy(
+                src_ref=lent_state_ref.at[origin, lent_cols(half)],
+                dst_ref=lent_state_ref.at[origin, lent_cols(half)],
+                send_sem=lent_sent_sem.at[3],
+                recv_sem=lent_state_sem.at[2],
+                device_id=(seq, to),
+                device_id_type=MESH,
+            ).start()
+
+    def settle(origin):
+        for at in range(SIZES[LENT]):
+            inter = jnp.dot(
+                lent_rows_ref[0, origin, :, head_cols(at)],
+                lent_state_ref[origin, head_cols(at), :],
+                preferred_element_type=F32,
+            )
+            attended = inter + lent_rows_ref[1, origin, :, head_cols(at)].astype(F32)
+            mean = jnp.sum(attended * attended, axis=-1, keepdims=True) * (1.0 / HD)
+            normed = attended * lax.rsqrt(mean + 1e-05) * lent_gain_ref[origin, at : at + 1, :]
+            cols = pl.ds(pl.multiple_of(origin * features + (FIRST[LENT] + at) * HD, HD), HD)
+            out_ref[:, cols] = normed.astype(BF16)
+
+    def settle_near():
+        wait_bytes(lent_picked_ref, lent_rows_sem.at[0])
+        wait_bytes(lent_gain_ref.at[pl.ds(0, head_count - 1)], lent_gain_sem.at[1])
+        settle(down)
+        settle(up)
+
+    def settle_far():
+        wait_bytes(lent_state_ref.at[0], lent_state_sem.at[2])
+        settle(far)
+
     def intra_group(g):
         for at in range(SIZES[g]):
             intra(FIRST[g] + at)
 
-    def states(g):
+    def wait_load(g):
         for copy in loads[g]:
             copy.wait()
+
+    def states(g):
         for at in range(SIZES[g]):
             state(FIRST[g] + at)
 
+    def make_decays():
+        for h in range(heads):
+            rate = rate_row(h, HD)
+            block_decay_ref[h] = jnp.broadcast_to(jnp.exp(-rate * length), (8, HD))
+            row_decay_ref[h] = jnp.broadcast_to(jnp.exp(-rate * (length * ROW)), (8, HD))
+
     level_load.wait()
+    wait_load(0)
     states(0)
-    pl.semaphore_wait(barrier, ROW - 1 + across - 1 + 2)
+    pl.semaphore_wait(barrier, ROW - 1 + across - 1 + 3)
     send_row(0)
+    q_load.wait()
+    lend(0)
+    wait_load(1)
     states(1)
     send_row(1)
+    make_pick()
+    lend_picked(0)
+    wait_load(2)
+    intra_group(2)
+    lend(1)
+    lend_picked(1)
     states(2)
     send_row(2)
+    wait_load(3)
     states(3)
     send_row(3)
-    for h in range(heads):
-        rate = rate_row(h, HD)
-        block_decay_ref[h] = jnp.broadcast_to(jnp.exp(-rate * length), (8, HD))
-        row_decay_ref[h] = jnp.broadcast_to(jnp.exp(-rate * (length * ROW)), (8, HD))
-    make_pick()
-    q_load.wait()
+    make_decays()
     gain_load.wait()
+    lend_gain()
+    sum_row(0)
+    wait_load(4)
     states(4)
     intra_group(0)
-    sum_row(0)
+    sum_row(1)
     intra_group(1)
-    sum_row(1)
-    intra_group(2)
+    lend_on(0)
     give_back(0)
     give_back(1)
     send_row(4)
     sum_row(2)
     sum_row(3)
     intra_group(3)
+    lend_on(1)
     give_back(2)
     finish(0)
     finish(1)
+    relay(0)
     give_back(3)
-    relay(0)
+    intra_group(4)
     relay(1)
     sum_row(4)
-    intra_group(4)
     finish(2)
+    finish(3)
     give_back(4)
-    finish(3)
-    relay(2)
+    lend_states_on()
+    relay(3)
     finish(4)
-    relay(3)
     relay(4)
+    settle_near()
+    settle_far()
 
     for g in range(GROUPS):
         wait_bytes(state_ref.at[others(g)], row_sem.at[0, g])
         wait_bytes(total_ref.at[pl.ds(0, across - 1), at_total(g)], total_sem.at[0, g])
         wait_bytes(back_ref.at[others(g)], back_sem.at[0, g])
-    wait_bytes(normed_ref, sent_sem.at[0])
-    wait_bytes(picked_ref, sent_sem.at[1])
-    wait_bytes(out_ref.at[:, pl.ds(0, 2 * features)], out_sem.at[0])
+    sent = features - lent_width
+    wait_bytes(normed_ref.at[:, pl.ds(0, sent)], sent_sem.at[0])
+    wait_bytes(picked_ref.at[:, :, pl.ds(0, sent // 2)], sent_sem.at[1])
+    wait_bytes(lent_ref, lent_sent_sem.at[0])
+    wait_bytes(lent_picked_ref, lent_sent_sem.at[1])
+    wait_bytes(lent_state_ref.at[pl.ds(0, 2)], lent_sent_sem.at[2])
+    wait_bytes(lent_state_ref.at[0], lent_sent_sem.at[3])
+    wait_bytes(lent_gain_ref.at[pl.ds(0, head_count - 1)], lent_gain_sem.at[0])
+    wait_bytes(out_ref.at[:, pl.ds(0, 2 * sent)], out_sem.at[0])
 
 
 def on_device(query, key_rows, value_rows, head_norm_gain, decay_level, routing):
@@ -384,6 +541,7 @@
     head_count = lax.axis_size("head")
     across = seq_count // ROW
     seats = EXPERTS // head_count * CAP
+    lent_width = SIZES[LENT] * HD
     outside = pl.BlockSpec(memory_space=pltpu.HBM)
     operands = [
         decay_level,
@@ -415,6 +573,12 @@
             pltpu.VMEM((2, length, features // 2), BF16),
             pltpu.VMEM((EXPERTS * CAP, length), BF16),
             pltpu.VMEM((4, seats, features // 2), BF16),
+            pltpu.VMEM((2, length, lent_width), BF16),
+            pltpu.VMEM((2, 2, length, lent_width // 2), BF16),
+            pltpu.VMEM((2, 4, seats, lent_width // 2), BF16),
+            pltpu.VMEM((2, head_count, seats, lent_width), BF16),
+            pltpu.VMEM((head_count, lent_width, HD), BF16),
+            pltpu.VMEM((head_count, 8, HD), F32),
             pltpu.VMEM((heads, 8, HD), F32),
             pltpu.VMEM((heads, 8, HD), F32),
             pltpu.SemaphoreType.DMA((4,)),
@@ -425,6 +589,11 @@
             pltpu.SemaphoreType.DMA((2, GROUPS)),
             pltpu.SemaphoreType.DMA((2,)),
             pltpu.SemaphoreType.DMA((1,)),
+            pltpu.SemaphoreType.DMA((2, 2)),
+            pltpu.SemaphoreType.DMA((4,)),
+            pltpu.SemaphoreType.DMA((1,)),
+            pltpu.SemaphoreType.DMA((3,)),
+            pltpu.SemaphoreType.DMA((2,)),
         ],
         compiler_params=pltpu.CompilerParams(
             collective_id=0, has_side_effects=True, vmem_limit_bytes=40 << 20

time: 56.4 us -> 53.6 us (0.950)
  Pallas kernels: 54.6 us -> 51.7 us
    pallas_call x1, Pallas kernels: 54.6 us -> 51.7 us  [on_device(): pl.pallas_call(functools.partial(kernel, (length, heads, seq_count, head_...]
where the time goes in v4:
time: 53.6 us; the launch traced here: 53.4 us
  Pallas kernels  51.7 us (96%)
  local copies, waits for them, and re-layouts  1.67 us (3%)
    pallas_call x1, Pallas kernels, on_device(): pl.pallas_call(functools.partial(kernel, (length, heads, seq_count, head_...  51.7 us
    unnamed x1, local copies, waits for them, and re-layouts  1.67 us

profile of v4, /device:TPU:1, one launch (start us, length us, event | category | flops | bytes accessed | tf_op | source)
XLA Modules:
  0.0 53.4 jit_solution(3809137946436889801)
XLA Ops:
  0.0 51.7 %attend_and_dispatch.1 = bf16[192,8192]{1,0:T(8,128)(2,1)S(1)} custom-call(s32[16]{0:T(128)} %level_hbm.1, s32[2,256]{1,0:T(2,128)} %bitcast.5, f32[16,128]{1,0:T(8,128)} %bitcast.4, bf16[256,2048]{1,0:T(8,128)(2,1)} %q_hbm.1, bf16[256,2048]{1,0:T(8,128)(2,1)} %k_hbm.1, bf16[256,2048]{1,0:T(8,128)(2,1)} %v_hbm.1), custom_call_target="tpu_custom_call" | custom-call | tf_op jit(solution)/shard_map/attend_and_dispatch/pallas_call | solution.py:554
  51.7 1.7 %copy.8 = bf16[8,24,8192]{2,1,0:T(8,128)(2,1)} copy(bf16[8,24,8192]{2,1,0:T(8,128)(2,1)S(1)} %bitcast.3) | data formatting | bytes 6291456

commit v5 on v4

--- a/solution.py
+++ b/solution.py
@@ -88,18 +88,20 @@
     loads = []
     for g in range(GROUPS):
         cols = pl.ds(FIRST[g] * HD, SIZES[g] * HD)
-        pair = [
-            pltpu.make_async_copy(k_hbm.at[:, cols], k_ref.at[:, cols], load_sem.at[0, g]),
-            pltpu.make_async_copy(v_hbm.at[:, cols], v_ref.at[:, cols], load_sem.at[1, g]),
-        ]
-        for copy in pair:
+        pairs = ((k_hbm, k_ref), (v_hbm, v_ref), (q_hbm, q_ref))
+        loads.append([
+            pltpu.make_async_copy(hbm.at[:, cols], ref.at[:, cols], load_sem.at[at, g])
+            for at, (hbm, ref) in enumerate(pairs)
+        ])
+    routing_load = pltpu.make_async_copy(routing_hbm, routing_ref, small_sem.at[1])
+    gain_load = pltpu.make_async_copy(gain_hbm, gain_ref, small_sem.at[2])
+    for copy in loads[0][:2]:
+        copy.start()
+    loads[LENT][2].start()
+    routing_load.start()
+    for g in range(GROUPS):
+        for copy in loads[g][2 * (g == 0) : 2 + (g != LENT)]:
             copy.start()
-        loads.append(pair)
-    routing_load = pltpu.make_async_copy(routing_hbm, routing_ref, small_sem.at[1])
-    routing_load.start()
-    q_load = pltpu.make_async_copy(q_hbm, q_ref, small_sem.at[2])
-    q_load.start()
-    gain_load = pltpu.make_async_copy(gain_hbm, gain_ref, small_sem.at[3])
     gain_load.start()
 
     barrier = pltpu.get_barrier_semaphore()
@@ -107,18 +109,18 @@
     def greet(device):
         pl.semaphore_signal(barrier, inc=1, device_id=device, device_id_type=MESH)
 
+    def far_first(i):
+        return ROW // 2 + lax.div(i + 1, 2) * (1 - 2 * lax.rem(i, 2))
+
     def row_peer(d):
         return lax.rem(me_row + d, ROW)
 
-    def far_first(i):
-        return ROW // 2 + lax.div(i + 1, 2) * (1 - 2 * lax.rem(i, 2))
-
     def x_peer(d):
         return lax.rem(me_x + d, across)
 
-    @pl.loop(1, ROW)
-    def _(d):
-        greet((row_base + row_peer(d), me_head))
+    @pl.loop(0, ROW - 1)
+    def _(i):
+        greet((row_base + row_peer(far_first(i)), me_head))
 
     for d in range(1, across):
         greet((x_peer(d) * ROW + me_row, me_head))
@@ -200,7 +202,7 @@
         for r in range(1, ROW):
             carried = decay * carried + rows_ref[member(g, r), :].astype(F32)
         total_ref[me_x, at_total(g)] = carried
-        for d in range(1, across):
+        for d in (across // 2, *(d for d in range(1, across) if d != across // 2)):
             total_copy(g, x_peer(d)).start()
 
     def back_copy(g, to):
@@ -314,6 +316,8 @@
                 normed_ref[:, head_cols(h)] = normed.astype(BF16)
             if g != LENT:
                 whole_copy(g, half).start()
+
+    def finish_picked(g):
         for half, to in () if g == LENT else ((1, up), (0, down)):
             picked_ref[half, :, packed_cols(g)] = picked_rows(to, normed_ref[:, half_cols(g, half)])
             send_picked(g, half, me_head, half, to)
@@ -367,6 +371,9 @@
                 else:
                     value = intra_ref[:, head_cols(h)]
                 lent_ref[part, :, head_cols(at)] = value.astype(BF16)
+
+    def lend_whole(part):
+        for half in range(2):
             lent_whole_copy(part, half).start()
 
     def lend_picked(part):
@@ -450,7 +457,7 @@
             intra(FIRST[g] + at)
 
     def wait_load(g):
-        for copy in loads[g]:
+        for copy in loads[g][:2]:
             copy.wait()
 
     def states(g):
@@ -466,10 +473,11 @@
     level_load.wait()
     wait_load(0)
     states(0)
+    loads[2][2].wait()
+    lend(0)
     pl.semaphore_wait(barrier, ROW - 1 + across - 1 + 3)
+    lend_whole(0)
     send_row(0)
-    q_load.wait()
-    lend(0)
     wait_load(1)
     states(1)
     send_row(1)
@@ -478,6 +486,7 @@
     wait_load(2)
     intra_group(2)
     lend(1)
+    lend_whole(1)
     lend_picked(1)
     states(2)
     send_row(2)
@@ -490,8 +499,10 @@
     sum_row(0)
     wait_load(4)
     states(4)
+    loads[0][2].wait()
     intra_group(0)
     sum_row(1)
+    loads[1][2].wait()
     intra_group(1)
     lend_on(0)
     give_back(0)
@@ -499,25 +510,32 @@
     send_row(4)
     sum_row(2)
     sum_row(3)
+    loads[3][2].wait()
     intra_group(3)
     lend_on(1)
     give_back(2)
     finish(0)
+    finish_picked(0)
     finish(1)
+    finish_picked(1)
+    give_back(3)
+    loads[4][2].wait()
+    intra_group(4)
     relay(0)
-    give_back(3)
-    intra_group(4)
-    relay(1)
     sum_row(4)
     finish(2)
+    finish_picked(2)
+    relay(1)
     finish(3)
+    finish_picked(3)
     give_back(4)
     lend_states_on()
     relay(3)
     finish(4)
-    relay(4)
+    finish_picked(4)
     settle_near()
     settle_far()
+    relay(4)
 
     for g in range(GROUPS):
         wait_bytes(state_ref.at[others(g)], row_sem.at[0, g])
@@ -581,8 +599,8 @@
             pltpu.VMEM((head_count, 8, HD), F32),
             pltpu.VMEM((heads, 8, HD), F32),
             pltpu.VMEM((heads, 8, HD), F32),
-            pltpu.SemaphoreType.DMA((4,)),
-            pltpu.SemaphoreType.DMA((2, GROUPS)),
+            pltpu.SemaphoreType.DMA((3,)),
+            pltpu.SemaphoreType.DMA((3, GROUPS)),
             pltpu.SemaphoreType.DMA((2, GROUPS)),
             pltpu.SemaphoreType.DMA((2, GROUPS)),
             pltpu.SemaphoreType.DMA((2, GROUPS)),

time: 53.6 us -> 53.5 us (level)
  no operation moved by 1% of the time
where the time goes in v5:
time: 53.5 us; the launch traced here: 53.2 us
  Pallas kernels  51.5 us (96%)
  local copies, waits for them, and re-layouts  1.67 us (3%)
    pallas_call x1, Pallas kernels, on_device(): pl.pallas_call(functools.partial(kernel, (length, heads, seq_count, head_...  51.5 us
    unnamed x1, local copies, waits for them, and re-layouts  1.67 us

profile of v5, /device:TPU:1, one launch (start us, length us, event | category | flops | bytes accessed | tf_op | source)
XLA Modules:
  0.0 53.2 jit_solution(15836310808358400471)
XLA Ops:
  0.0 51.5 %attend_and_dispatch.1 = bf16[192,8192]{1,0:T(8,128)(2,1)S(1)} custom-call(s32[16]{0:T(128)} %level_hbm.1, s32[2,256]{1,0:T(2,128)} %bitcast.5, f32[16,128]{1,0:T(8,128)} %bitcast.4, bf16[256,2048]{1,0:T(8,128)(2,1)} %q_hbm.1, bf16[256,2048]{1,0:T(8,128)(2,1)} %k_hbm.1, bf16[256,2048]{1,0:T(8,128)(2,1)} %v_hbm.1), custom_call_target="tpu_custom_call" | custom-call | tf_op jit(solution)/shard_map/attend_and_dispatch/pallas_call | solution.py:572
  51.6 1.7 %copy.8 = bf16[8,24,8192]{2,1,0:T(8,128)(2,1)} copy(bf16[8,24,8192]{2,1,0:T(8,128)(2,1)S(1)} %bitcast.3) | data formatting | bytes 6291456

commit v6 on v5

--- a/solution.py
+++ b/solution.py
@@ -533,9 +533,9 @@
     relay(3)
     finish(4)
     finish_picked(4)
+    relay(4)
     settle_near()
     settle_far()
-    relay(4)
 
     for g in range(GROUPS):
         wait_bytes(state_ref.at[others(g)], row_sem.at[0, g])

time: 53.5 us -> 53.5 us (level)
  no operation moved by 1% of the time
where the time goes in v6:
time: 53.5 us; the launch traced here: 53.2 us
  Pallas kernels  51.5 us (96%)
  local copies, waits for them, and re-layouts  1.67 us (3%)
    pallas_call x1, Pallas kernels, on_device(): pl.pallas_call(functools.partial(kernel, (length, heads, seq_count, head_...  51.5 us
    unnamed x1, local copies, waits for them, and re-layouts  1.67 us

profile of v6, /device:TPU:1, one launch (start us, length us, event | category | flops | bytes accessed | tf_op | source)
XLA Modules:
  0.0 53.2 jit_solution(12543851341079383968)
XLA Ops:
  0.0 51.5 %attend_and_dispatch.1 = bf16[192,8192]{1,0:T(8,128)(2,1)S(1)} custom-call(s32[16]{0:T(128)} %level_hbm.1, s32[2,256]{1,0:T(2,128)} %bitcast.5, f32[16,128]{1,0:T(8,128)} %bitcast.4, bf16[256,2048]{1,0:T(8,128)(2,1)} %q_hbm.1, bf16[256,2048]{1,0:T(8,128)(2,1)} %k_hbm.1, bf16[256,2048]{1,0:T(8,128)(2,1)} %v_hbm.1), custom_call_target="tpu_custom_call" | custom-call | tf_op jit(solution)/shard_map/attend_and_dispatch/pallas_call | solution.py:572
  51.6 1.7 %copy.8 = bf16[8,24,8192]{2,1,0:T(8,128)(2,1)} copy(bf16[8,24,8192]{2,1,0:T(8,128)(2,1)S(1)} %bitcast.3) | data formatting | bytes 6291456
